TPU v7x, 256 devices: a whole 4x4x8 slice. The times are simulated.
256 devices in a mesh: head: 8 (over z_lo, core), blk: 32 (over y, x, z_hi).
Axes of the slice: x: 4, y: 4, z: 8 (z_hi: 2, z_lo: 4; z = z_hi * 4 + z_lo), core: 2. Of those that a mesh axis runs over, the one named last changes fastest.
Arguments:
- query_act: bfloat16 [8192, 5120], P(('blk', 'head')), may hold values from -6 to 6
- key_act: bfloat16 [8192, 1024], P(('blk', 'head')), may hold values from -6 to 6
- value_act: bfloat16 [8192, 1024], P(('blk', 'head')), may hold values from -6 to 6
- attn_out: bfloat16 [8192, 5120], P(('blk', 'head')), may hold values from -4 to 4
- grad_out: bfloat16 [8192, 5120], P(('blk', 'head')), may hold values from -6 to 6
- log_sum: float32 [8192, 40], P(('blk', 'head')), may hold values from 5 to 6.5
- kv_lists: int32 [64, 32], P('blk'), may hold values from -1 to 63, as said below
Outputs:
- grad_query: bfloat16 [8192, 5120], P(('blk', 'head'))
- grad_key: bfloat16 [8192, 1024], P(('blk', 'head'))
- grad_value: bfloat16 [8192, 1024], P(('blk', 'head'))
Inputs may be any that keep to these rules, and one draw needn't show every extreme that they name: `kv_lists`: the pack is made of prompt trees: the first holds 16 blocks, the last 16, and those between 32 blocks each, in order. A tree is a prompt, then branches. Row r names in rising order the blocks whose keys block r sees (the tree's prompt blocks up to r, and the earlier blocks of r's branch), then -1 to the end. Every entry lies in the same tree as r and is at most r; r itself is always named.
All inputs are finite; a program needn't handle non-finite values.
Results may differ from a plain program's by a relative error of at most 0.0049.
Values may be sent and summed in bfloat16 or wider, within the bound.
A program may use at most 64 MiB of HBM per device.

v0:
```python
import jax
import jax.numpy as jnp
from jax import lax
from jax.sharding import PartitionSpec as P

QH = 40
KVH = 8
HD = 128
BLOCK = 128


def passed_along(array, axis, by):
    size = lax.axis_size(axis)
    pairs = [(i, i + by) for i in range(size) if 0 <= i + by < size]
    return lax.ppermute(array, axis, pairs)


def shifted(array, axis, by):
    size = lax.axis_size(axis)
    return lax.ppermute(array, axis, [(i, (i + by) % size) for i in range(size)])


def head_delta(grad_rows, out_rows, heads):
    count = grad_rows.shape[0]
    return jnp.einsum(
        "thd,thd->th",
        grad_rows.reshape(count, heads, HD),
        out_rows.reshape(count, heads, HD),
        preferred_element_type=jnp.float32,
    )


def local(query_act, key_act, value_act, attn_out, grad_out, log_sum, kv_lists):
    head_count = lax.axis_size("head")
    blk_count = lax.axis_size("blk")
    query_rows, key_rows, value_rows, grad_rows, total_rows, out_rows = (
        lax.all_to_all(
            query_act.astype(jnp.float32), "head", split_axis=1, concat_axis=0, tiled=True
        ).astype(query_act.dtype),
        lax.all_to_all(
            key_act.astype(jnp.float32), "head", split_axis=1, concat_axis=0, tiled=True
        ).astype(key_act.dtype),
        lax.all_to_all(
            value_act.astype(jnp.float32), "head", split_axis=1, concat_axis=0, tiled=True
        ).astype(value_act.dtype),
        lax.all_to_all(
            grad_out.astype(jnp.float32), "head", split_axis=1, concat_axis=0, tiled=True
        ).astype(grad_out.dtype),
        lax.all_to_all(log_sum, "head", split_axis=1, concat_axis=0, tiled=True),
        lax.all_to_all(
            attn_out.astype(jnp.float32), "head", split_axis=1, concat_axis=0, tiled=True
        ).astype(attn_out.dtype),
    )
    delta_rows = head_delta(grad_rows, out_rows, QH // head_count)
    tokens = query_rows.shape[0]
    local_heads = KVH // head_count
    group_size = QH // KVH
    blocks_dev = tokens // BLOCK
    scaling = HD ** (-0.5)
    queries = query_rows.reshape(tokens, local_heads, group_size, HD)
    out_grads = grad_rows.reshape(tokens, local_heads, group_size, HD)
    row_totals = total_rows.reshape(tokens, local_heads, group_size).transpose(1, 2, 0)[
        :, :, :, None
    ]
    row_deltas = delta_rows.reshape(tokens, local_heads, group_size).transpose(1, 2, 0)[
        :, :, :, None
    ]
    position = lax.axis_index("blk")
    query_pos = position * tokens + jnp.arange(tokens, dtype=jnp.int32)

    def block_mask(rotation):
        source = (position - rotation) % blk_count
        key_ids = source * blocks_dev + jnp.arange(blocks_dev, dtype=jnp.int32)
        listed = jnp.any(kv_lists[:, :, None] == key_ids[None, None, :], axis=1)
        key_pos = source * tokens + jnp.arange(tokens, dtype=jnp.int32)
        return (listed, key_pos)

    def attend(kv_pair, key_sums, query_grad, listed, key_pos):
        visible = jnp.repeat(jnp.repeat(listed, BLOCK, axis=0), BLOCK, axis=1) & (
            key_pos[None, :] <= query_pos[:, None]
        )
        key_block = kv_pair[0].reshape(tokens, local_heads, HD)
        value_block = kv_pair[1].reshape(tokens, local_heads, HD)
        scores = (
            jnp.einsum("tkgd,skd->kgts", queries, key_block, preferred_element_type=jnp.float32)
            * scaling
        )
        weights = jnp.where(visible, jnp.exp(scores - row_totals), 0.0)
        grad_probs = jnp.einsum(
            "tkgd,skd->kgts", out_grads, value_block, preferred_element_type=jnp.float32
        )
        grad_scores = (weights * (grad_probs - row_deltas)).astype(jnp.bfloat16)
        probs_low = weights.astype(jnp.bfloat16)
        value_part = jnp.einsum(
            "kgts,tkgd->skd", probs_low, out_grads, preferred_element_type=jnp.float32
        )
        key_part = (
            jnp.einsum("kgts,tkgd->skd", grad_scores, queries, preferred_element_type=jnp.float32)
            * scaling
        )
        query_part = (
            jnp.einsum("kgts,skd->tkgd", grad_scores, key_block, preferred_element_type=jnp.float32)
            * scaling
        )
        added = jnp.stack(
            [
                key_part.reshape(tokens, local_heads * HD),
                value_part.reshape(tokens, local_heads * HD),
            ]
        )
        return (key_sums + added, query_grad + query_part)

    def visit(rotation, kv_pair, key_sums, query_grad):
        listed, key_pos = block_mask(rotation)
        return attend(kv_pair, key_sums, query_grad, listed, key_pos)

    kv_pair = jnp.stack([key_rows, value_rows])
    empty_sums = jnp.zeros((2, tokens, local_heads * HD), jnp.float32)
    empty_grad = jnp.zeros((tokens, local_heads, group_size, HD), jnp.float32)

    def advance(rotation, carried):
        kv_here, key_sums, query_grad = carried
        arrived = passed_along(kv_here, "blk", 1)
        key_sums, query_grad = visit(rotation, kv_here, key_sums, query_grad)
        key_sums = shifted(key_sums, "blk", 1)
        return (arrived, key_sums, query_grad)

    kv_here, key_sums, query_grad = lax.fori_loop(
        0, blk_count - 1, advance, (kv_pair, empty_sums, empty_grad)
    )
    key_sums, query_grad = visit(blk_count - 1, kv_here, key_sums, query_grad)
    key_sums = shifted(key_sums.astype(jnp.bfloat16), "blk", 1 - blk_count).astype(key_sums.dtype)
    query_low = query_grad.reshape(tokens, local_heads * group_size * HD).astype(jnp.bfloat16)
    key_low = key_sums[0].astype(jnp.bfloat16)
    value_low = key_sums[1].astype(jnp.bfloat16)
    grad_query, grad_key, grad_value = (
        lax.all_to_all(query_low, "head", split_axis=0, concat_axis=1, tiled=True),
        lax.all_to_all(key_low, "head", split_axis=0, concat_axis=1, tiled=True),
        lax.all_to_all(value_low, "head", split_axis=0, concat_axis=1, tiled=True),
    )
    return (grad_query, grad_key, grad_value)


def solution(mesh):
    return jax.shard_map(
        local,
        mesh=mesh,
        in_specs=(
            P(("blk", "head"), None),
            P(("blk", "head"), None),
            P(("blk", "head"), None),
            P(("blk", "head"), None),
            P(("blk", "head"), None),
            P(("blk", "head"), None),
            P("blk", None),
        ),
        out_specs=(P(("blk", "head"), None), P(("blk", "head"), None), P(("blk", "head"), None)),
        check_vma=False,
    )
```

profile of v0, /device:TPU:1, one launch (start us, length us, event | category | flops | bytes accessed | tf_op | source)
XLA Modules:
  0.0 885.4 jit_solution(12147705580826864450)
XLA Ops:
  37.8 9.3 %all-to-all-done.2 = bf16[32,8,640]{2,0,1:T(8,128)(2,1)S(1)} async-done(((bf16[32,8,640]{2,0,1:T(8,128)(2,1)}), bf16[32,8,640]{2,0,1:T(8,128)(2,1)S(1)}, u32[]{:S(2)}, u32[]{:S(2)}) %all-to-all-start.2) | async-done | bytes 327712 | tf_op jit(solution)/shard_map/all_to_all | solution.py:37
  78.6 715.4 %while.20 = (s32[]{:T(128)}, bf16[2,256,128]{2,1,0:T(8,128)(2,1)S(1)}, f32[2,256,128]{2,1,0:T(8,128)S(1)}, f32[256,1,5,128]{3,0,2,1:T(8,128)S(1)}, s32[2,32]{1,0...) while((s32[]{:T(128)}, ...), condition=%wide.region_2.3_spmd.clone, body=%wide.region_0.2_spmd.clone.sunk | while | flops 422511360 | bytes 11754164 | solution.py:128
  89.5 17.8 %collective-permute-done.1 = f32[2,256,128]{2,1,0:T(8,128)S(1)} collective-permute-done((f32[2,256,128]{2,1,0:T(8,128)S(1)}, f32[2,256,128]{2,1,0:T(8,128)S(1)}, u32[]{:S(2)}, u32[]{:S(2)}) %collective-permute-start.1) | collective-permute-done | bytes 262176 | tf_op jit(solution)/shard_map/while/body/eval_jaxpr/ppermute | solution.py:20
  111.3 15.7 %collective-permute-done.1 = f32[2,256,128]{2,1,0:T(8,128)S(1)} collective-permute-done((f32[2,256,128]{2,1,0:T(8,128)S(1)}, f32[2,256,128]{2,1,0:T(8,128)S(1)}, u32[]{:S(2)}, u32[]{:S(2)}) %collective-permute-start.1) | collective-permute-done | bytes 262176 | tf_op jit(solution)/shard_map/while/body/eval_jaxpr/ppermute | solution.py:20
  132.3 11.8 %collective-permute-done.1 = f32[2,256,128]{2,1,0:T(8,128)S(1)} collective-permute-done((f32[2,256,128]{2,1,0:T(8,128)S(1)}, f32[2,256,128]{2,1,0:T(8,128)S(1)}, u32[]{:S(2)}, u32[]{:S(2)}) %collective-permute-start.1) | collective-permute-done | bytes 262176 | tf_op jit(solution)/shard_map/while/body/eval_jaxpr/ppermute | solution.py:20
  160.9 10.9 %collective-permute-start = (bf16[2,256,128]{2,1,0:T(8,128)(2,1)S(1)}, bf16[2,256,128]{2,1,0:T(8,128)(2,1)S(1)}, u32[]{:S(2)}, u32[]{:S(2)}) collective-permute-start(bf16[2,256,128]{2,1,0:T(8,128)(2,1)S(1)} %copy.135), channel_id=1, source_target_pairs={{0,1},{1,2},{2,3},{3,4},{4,5},{5,6},{6,7},{7,8},{8,9},{9,10},{10,1... | collective-permute-start | bytes 393224 | tf_op jit(solution)/shard_map/while/body/eval_jaxpr/ppermute | solution.py:15
  201.5 13.4 %collective-permute-done.1 = f32[2,256,128]{2,1,0:T(8,128)S(1)} collective-permute-done((f32[2,256,128]{2,1,0:T(8,128)S(1)}, f32[2,256,128]{2,1,0:T(8,128)S(1)}, u32[]{:S(2)}, u32[]{:S(2)}) %collective-permute-start.1) | collective-permute-done | bytes 262176 | tf_op jit(solution)/shard_map/while/body/eval_jaxpr/ppermute | solution.py:20
  219.4 13.7 %collective-permute-done.1 = f32[2,256,128]{2,1,0:T(8,128)S(1)} collective-permute-done((f32[2,256,128]{2,1,0:T(8,128)S(1)}, f32[2,256,128]{2,1,0:T(8,128)S(1)}, u32[]{:S(2)}, u32[]{:S(2)}) %collective-permute-start.1) | collective-permute-done | bytes 262176 | tf_op jit(solution)/shard_map/while/body/eval_jaxpr/ppermute | solution.py:20
  237.8 13.6 %collective-permute-done.1 = f32[2,256,128]{2,1,0:T(8,128)S(1)} collective-permute-done((f32[2,256,128]{2,1,0:T(8,128)S(1)}, f32[2,256,128]{2,1,0:T(8,128)S(1)}, u32[]{:S(2)}, u32[]{:S(2)}) %collective-permute-start.1) | collective-permute-done | bytes 262176 | tf_op jit(solution)/shard_map/while/body/eval_jaxpr/ppermute | solution.py:20
  259.7 17.5 %collective-permute-done.1 = f32[2,256,128]{2,1,0:T(8,128)S(1)} collective-permute-done((f32[2,256,128]{2,1,0:T(8,128)S(1)}, f32[2,256,128]{2,1,0:T(8,128)S(1)}, u32[]{:S(2)}, u32[]{:S(2)}) %collective-permute-start.1) | collective-permute-done | bytes 262176 | tf_op jit(solution)/shard_map/while/body/eval_jaxpr/ppermute | solution.py:20
  285.8 10.4 %collective-permute-done.1 = f32[2,256,128]{2,1,0:T(8,128)S(1)} collective-permute-done((f32[2,256,128]{2,1,0:T(8,128)S(1)}, f32[2,256,128]{2,1,0:T(8,128)S(1)}, u32[]{:S(2)}, u32[]{:S(2)}) %collective-permute-start.1) | collective-permute-done | bytes 262176 | tf_op jit(solution)/shard_map/while/body/eval_jaxpr/ppermute | solution.py:20
  303.1 16.4 %collective-permute-done.1 = f32[2,256,128]{2,1,0:T(8,128)S(1)} collective-permute-done((f32[2,256,128]{2,1,0:T(8,128)S(1)}, f32[2,256,128]{2,1,0:T(8,128)S(1)}, u32[]{:S(2)}, u32[]{:S(2)}) %collective-permute-start.1) | collective-permute-done | bytes 262176 | tf_op jit(solution)/shard_map/while/body/eval_jaxpr/ppermute | solution.py:20
  324.6 11.9 %collective-permute-done.1 = f32[2,256,128]{2,1,0:T(8,128)S(1)} collective-permute-done((f32[2,256,128]{2,1,0:T(8,128)S(1)}, f32[2,256,128]{2,1,0:T(8,128)S(1)}, u32[]{:S(2)}, u32[]{:S(2)}) %collective-permute-start.1) | collective-permute-done | bytes 262176 | tf_op jit(solution)/shard_map/while/body/eval_jaxpr/ppermute | solution.py:20
  347.2 9.1 %collective-permute-done.1 = f32[2,256,128]{2,1,0:T(8,128)S(1)} collective-permute-done((f32[2,256,128]{2,1,0:T(8,128)S(1)}, f32[2,256,128]{2,1,0:T(8,128)S(1)}, u32[]{:S(2)}, u32[]{:S(2)}) %collective-permute-start.1) | collective-permute-done | bytes 262176 | tf_op jit(solution)/shard_map/while/body/eval_jaxpr/ppermute | solution.py:20
  359.8 10.7 %collective-permute-start.1 = (f32[2,256,128]{2,1,0:T(8,128)S(1)}, f32[2,256,128]{2,1,0:T(8,128)S(1)}, u32[]{:S(2)}, u32[]{:S(2)}) collective-permute-start(f32[2,256,128]{2,1,0:T(8,128)S(1)} %maximum_add_fusion.3), channel_id=1, source_target_pairs={{0,1},{1,2},{2,3},{3,4},{4,5},{5,6},{6,7},{7,8},{8,9},{9,10},{10,1... | collective-permute-start | bytes 786440 | tf_op jit(solution)/shard_map/while/body/eval_jaxpr/ppermute | solution.py:20
  378.1 12.3 %collective-permute-start = (bf16[2,256,128]{2,1,0:T(8,128)(2,1)S(1)}, bf16[2,256,128]{2,1,0:T(8,128)(2,1)S(1)}, u32[]{:S(2)}, u32[]{:S(2)}) collective-permute-start(bf16[2,256,128]{2,1,0:T(8,128)(2,1)S(1)} %copy.135), channel_id=1, source_target_pairs={{0,1},{1,2},{2,3},{3,4},{4,5},{5,6},{6,7},{7,8},{8,9},{9,10},{10,1... | collective-permute-start | bytes 393224 | tf_op jit(solution)/shard_map/while/body/eval_jaxpr/ppermute | solution.py:15
  400.0 12.3 %collective-permute-done.1 = f32[2,256,128]{2,1,0:T(8,128)S(1)} collective-permute-done((f32[2,256,128]{2,1,0:T(8,128)S(1)}, f32[2,256,128]{2,1,0:T(8,128)S(1)}, u32[]{:S(2)}, u32[]{:S(2)}) %collective-permute-start.1) | collective-permute-done | bytes 262176 | tf_op jit(solution)/shard_map/while/body/eval_jaxpr/ppermute | solution.py:20
  422.7 9.8 %collective-permute-done.1 = f32[2,256,128]{2,1,0:T(8,128)S(1)} collective-permute-done((f32[2,256,128]{2,1,0:T(8,128)S(1)}, f32[2,256,128]{2,1,0:T(8,128)S(1)}, u32[]{:S(2)}, u32[]{:S(2)}) %collective-permute-start.1) | collective-permute-done | bytes 262176 | tf_op jit(solution)/shard_map/while/body/eval_jaxpr/ppermute | solution.py:20
  432.5 16.5 %collective-permute-start = (bf16[2,256,128]{2,1,0:T(8,128)(2,1)S(1)}, bf16[2,256,128]{2,1,0:T(8,128)(2,1)S(1)}, u32[]{:S(2)}, u32[]{:S(2)}) collective-permute-start(bf16[2,256,128]{2,1,0:T(8,128)(2,1)S(1)} %copy.135), channel_id=1, source_target_pairs={{0,1},{1,2},{2,3},{3,4},{4,5},{5,6},{6,7},{7,8},{8,9},{9,10},{10,1... | collective-permute-start | bytes 393224 | tf_op jit(solution)/shard_map/while/body/eval_jaxpr/ppermute | solution.py:15
  458.7 10.2 %collective-permute-done.1 = f32[2,256,128]{2,1,0:T(8,128)S(1)} collective-permute-done((f32[2,256,128]{2,1,0:T(8,128)S(1)}, f32[2,256,128]{2,1,0:T(8,128)S(1)}, u32[]{:S(2)}, u32[]{:S(2)}) %collective-permute-start.1) | collective-permute-done | bytes 262176 | tf_op jit(solution)/shard_map/while/body/eval_jaxpr/ppermute | solution.py:20
  476.6 9.1 %collective-permute-done.1 = f32[2,256,128]{2,1,0:T(8,128)S(1)} collective-permute-done((f32[2,256,128]{2,1,0:T(8,128)S(1)}, f32[2,256,128]{2,1,0:T(8,128)S(1)}, u32[]{:S(2)}, u32[]{:S(2)}) %collective-permute-start.1) | collective-permute-done | bytes 262176 | tf_op jit(solution)/shard_map/while/body/eval_jaxpr/ppermute | solution.py:20
  494.7 10.8 %collective-permute-done.1 = f32[2,256,128]{2,1,0:T(8,128)S(1)} collective-permute-done((f32[2,256,128]{2,1,0:T(8,128)S(1)}, f32[2,256,128]{2,1,0:T(8,128)S(1)}, u32[]{:S(2)}, u32[]{:S(2)}) %collective-permute-start.1) | collective-permute-done | bytes 262176 | tf_op jit(solution)/shard_map/while/body/eval_jaxpr/ppermute | solution.py:20
  530.7 13.6 %collective-permute-start.1 = (f32[2,256,128]{2,1,0:T(8,128)S(1)}, f32[2,256,128]{2,1,0:T(8,128)S(1)}, u32[]{:S(2)}, u32[]{:S(2)}) collective-permute-start(f32[2,256,128]{2,1,0:T(8,128)S(1)} %maximum_add_fusion.3), channel_id=1, source_target_pairs={{0,1},{1,2},{2,3},{3,4},{4,5},{5,6},{6,7},{7,8},{8,9},{9,10},{10,1... | collective-permute-start | bytes 786440 | tf_op jit(solution)/shard_map/while/body/eval_jaxpr/ppermute | solution.py:20
  548.1 10.0 %collective-permute-start = (bf16[2,256,128]{2,1,0:T(8,128)(2,1)S(1)}, bf16[2,256,128]{2,1,0:T(8,128)(2,1)S(1)}, u32[]{:S(2)}, u32[]{:S(2)}) collective-permute-start(bf16[2,256,128]{2,1,0:T(8,128)(2,1)S(1)} %copy.135), channel_id=1, source_target_pairs={{0,1},{1,2},{2,3},{3,4},{4,5},{5,6},{6,7},{7,8},{8,9},{9,10},{10,1... | collective-permute-start | bytes 393224 | tf_op jit(solution)/shard_map/while/body/eval_jaxpr/ppermute | solution.py:15
  581.3 9.9 %collective-permute-start.1 = (f32[2,256,128]{2,1,0:T(8,128)S(1)}, f32[2,256,128]{2,1,0:T(8,128)S(1)}, u32[]{:S(2)}, u32[]{:S(2)}) collective-permute-start(f32[2,256,128]{2,1,0:T(8,128)S(1)} %maximum_add_fusion.3), channel_id=1, source_target_pairs={{0,1},{1,2},{2,3},{3,4},{4,5},{5,6},{6,7},{7,8},{8,9},{9,10},{10,1... | collective-permute-start | bytes 786440 | tf_op jit(solution)/shard_map/while/body/eval_jaxpr/ppermute | solution.py:20
  682.5 10.8 %collective-permute-done.1 = f32[2,256,128]{2,1,0:T(8,128)S(1)} collective-permute-done((f32[2,256,128]{2,1,0:T(8,128)S(1)}, f32[2,256,128]{2,1,0:T(8,128)S(1)}, u32[]{:S(2)}, u32[]{:S(2)}) %collective-permute-start.1) | collective-permute-done | bytes 262176 | tf_op jit(solution)/shard_map/while/body/eval_jaxpr/ppermute | solution.py:20
  702.9 12.1 %collective-permute-done.1 = f32[2,256,128]{2,1,0:T(8,128)S(1)} collective-permute-done((f32[2,256,128]{2,1,0:T(8,128)S(1)}, f32[2,256,128]{2,1,0:T(8,128)S(1)}, u32[]{:S(2)}, u32[]{:S(2)}) %collective-permute-start.1) | collective-permute-done | bytes 262176 | tf_op jit(solution)/shard_map/while/body/eval_jaxpr/ppermute | solution.py:20
  728.5 15.6 %collective-permute-done.1 = f32[2,256,128]{2,1,0:T(8,128)S(1)} collective-permute-done((f32[2,256,128]{2,1,0:T(8,128)S(1)}, f32[2,256,128]{2,1,0:T(8,128)S(1)}, u32[]{:S(2)}, u32[]{:S(2)}) %collective-permute-start.1) | collective-permute-done | bytes 262176 | tf_op jit(solution)/shard_map/while/body/eval_jaxpr/ppermute | solution.py:20
  753.2 9.8 %collective-permute-done.1 = f32[2,256,128]{2,1,0:T(8,128)S(1)} collective-permute-done((f32[2,256,128]{2,1,0:T(8,128)S(1)}, f32[2,256,128]{2,1,0:T(8,128)S(1)}, u32[]{:S(2)}, u32[]{:S(2)}) %collective-permute-start.1) | collective-permute-done | bytes 262176 | tf_op jit(solution)/shard_map/while/body/eval_jaxpr/ppermute | solution.py:20
  777.3 16.6 %collective-permute-done.1 = f32[2,256,128]{2,1,0:T(8,128)S(1)} collective-permute-done((f32[2,256,128]{2,1,0:T(8,128)S(1)}, f32[2,256,128]{2,1,0:T(8,128)S(1)}, u32[]{:S(2)}, u32[]{:S(2)}) %collective-permute-start.1) | collective-permute-done | bytes 262176 | tf_op jit(solution)/shard_map/while/body/eval_jaxpr/ppermute | solution.py:20
  797.3 13.5 %collective-permute-done.2 = bf16[2,256,128]{2,1,0:T(8,128)(2,1)S(1)} collective-permute-done((bf16[2,256,128]{2,1,0:T(8,128)(2,1)S(1)}, bf16[2,256,128]{2,1,0:T(8,128)(2,1)S(1)}, u32[]{:S(2)}, u32[]{:S(2)}) %collective-permute-start.2) | collective-permute-done | bytes 131104 | tf_op jit(solution)/shard_map/ppermute | solution.py:20
  811.4 44.8 %all-to-all-start.7 = ((bf16[8,32,128]{2,1,0:T(8,128)(2,1)}), bf16[8,32,128]{2,1,0:T(8,128)(2,1)S(1)}, u32[]{:S(2)}, u32[]{:S(2)}) async-start(bf16[8,32,128]{2,1,0:T(8,128)(2,1)} %bitcast.41), calls=%async_computation.7 | async-start | bytes 131072 | tf_op jit(solution)/shard_map/all_to_all | solution.py:138
  (634 shorter events, 461.0 us)
Async XLA Ops:
  61.6 15.2 %all-to-all-start.5 = ((bf16[32,8,640]{2,0,1:T(8,128)(2,1)}), bf16[32,8,640]{2,0,1:T(8,128)(2,1)}, u32[]{:S(2)}, u32[]{:S(2)}) async-start(bf16[32,8,640]{2,0,1:T(8,128)(2,1)} %bitcast.251), calls=%async_computation.5 | async-start | bytes 655360 | tf_op jit(solution)/shard_map/all_to_all | solution.py:50
  86.9 20.5 %collective-permute-start.1 = (f32[2,256,128]{2,1,0:T(8,128)S(1)}, f32[2,256,128]{2,1,0:T(8,128)S(1)}, u32[]{:S(2)}, u32[]{:S(2)}) collective-permute-start(f32[2,256,128]{2,1,0:T(8,128)S(1)} %maximum_add_fusion.3), channel_id=1, source_target_pairs={{0,1},{1,2},{2,3},{3,4},{4,5},{5,6},{6,7},{7,8},{8,9},{9,10},{10,1... | collective-permute-start | bytes 786440 | tf_op jit(solution)/shard_map/while/body/eval_jaxpr/ppermute | solution.py:20
  110.7 16.3 %collective-permute-start.1 = (f32[2,256,128]{2,1,0:T(8,128)S(1)}, f32[2,256,128]{2,1,0:T(8,128)S(1)}, u32[]{:S(2)}, u32[]{:S(2)}) collective-permute-start(f32[2,256,128]{2,1,0:T(8,128)S(1)} %maximum_add_fusion.3), channel_id=1, source_target_pairs={{0,1},{1,2},{2,3},{3,4},{4,5},{5,6},{6,7},{7,8},{8,9},{9,10},{10,1... | collective-permute-start | bytes 786440 | tf_op jit(solution)/shard_map/while/body/eval_jaxpr/ppermute | solution.py:20
  160.9 20.7 %collective-permute-start = (bf16[2,256,128]{2,1,0:T(8,128)(2,1)S(1)}, bf16[2,256,128]{2,1,0:T(8,128)(2,1)S(1)}, u32[]{:S(2)}, u32[]{:S(2)}) collective-permute-start(bf16[2,256,128]{2,1,0:T(8,128)(2,1)S(1)} %copy.135), channel_id=1, source_target_pairs={{0,1},{1,2},{2,3},{3,4},{4,5},{5,6},{6,7},{7,8},{8,9},{9,10},{10,1... | collective-permute-start | bytes 393224 | tf_op jit(solution)/shard_map/while/body/eval_jaxpr/ppermute | solution.py:15
  196.8 18.1 %collective-permute-start.1 = (f32[2,256,128]{2,1,0:T(8,128)S(1)}, f32[2,256,128]{2,1,0:T(8,128)S(1)}, u32[]{:S(2)}, u32[]{:S(2)}) collective-permute-start(f32[2,256,128]{2,1,0:T(8,128)S(1)} %maximum_add_fusion.3), channel_id=1, source_target_pairs={{0,1},{1,2},{2,3},{3,4},{4,5},{5,6},{6,7},{7,8},{8,9},{9,10},{10,1... | collective-permute-start | bytes 786440 | tf_op jit(solution)/shard_map/while/body/eval_jaxpr/ppermute | solution.py:20
  254.7 22.4 %collective-permute-start.1 = (f32[2,256,128]{2,1,0:T(8,128)S(1)}, f32[2,256,128]{2,1,0:T(8,128)S(1)}, u32[]{:S(2)}, u32[]{:S(2)}) collective-permute-start(f32[2,256,128]{2,1,0:T(8,128)S(1)} %maximum_add_fusion.3), channel_id=1, source_target_pairs={{0,1},{1,2},{2,3},{3,4},{4,5},{5,6},{6,7},{7,8},{8,9},{9,10},{10,1... | collective-permute-start | bytes 786440 | tf_op jit(solution)/shard_map/while/body/eval_jaxpr/ppermute | solution.py:20
  280.5 15.7 %collective-permute-start.1 = (f32[2,256,128]{2,1,0:T(8,128)S(1)}, f32[2,256,128]{2,1,0:T(8,128)S(1)}, u32[]{:S(2)}, u32[]{:S(2)}) collective-permute-start(f32[2,256,128]{2,1,0:T(8,128)S(1)} %maximum_add_fusion.3), channel_id=1, source_target_pairs={{0,1},{1,2},{2,3},{3,4},{4,5},{5,6},{6,7},{7,8},{8,9},{9,10},{10,1... | collective-permute-start | bytes 786440 | tf_op jit(solution)/shard_map/while/body/eval_jaxpr/ppermute | solution.py:20
  301.5 18.1 %collective-permute-start.1 = (f32[2,256,128]{2,1,0:T(8,128)S(1)}, f32[2,256,128]{2,1,0:T(8,128)S(1)}, u32[]{:S(2)}, u32[]{:S(2)}) collective-permute-start(f32[2,256,128]{2,1,0:T(8,128)S(1)} %maximum_add_fusion.3), channel_id=1, source_target_pairs={{0,1},{1,2},{2,3},{3,4},{4,5},{5,6},{6,7},{7,8},{8,9},{9,10},{10,1... | collective-permute-start | bytes 786440 | tf_op jit(solution)/shard_map/while/body/eval_jaxpr/ppermute | solution.py:20
  359.8 18.3 %collective-permute-start.1 = (f32[2,256,128]{2,1,0:T(8,128)S(1)}, f32[2,256,128]{2,1,0:T(8,128)S(1)}, u32[]{:S(2)}, u32[]{:S(2)}) collective-permute-start(f32[2,256,128]{2,1,0:T(8,128)S(1)} %maximum_add_fusion.3), channel_id=1, source_target_pairs={{0,1},{1,2},{2,3},{3,4},{4,5},{5,6},{6,7},{7,8},{8,9},{9,10},{10,1... | collective-permute-start | bytes 786440 | tf_op jit(solution)/shard_map/while/body/eval_jaxpr/ppermute | solution.py:20
  378.1 21.9 %collective-permute-start = (bf16[2,256,128]{2,1,0:T(8,128)(2,1)S(1)}, bf16[2,256,128]{2,1,0:T(8,128)(2,1)S(1)}, u32[]{:S(2)}, u32[]{:S(2)}) collective-permute-start(bf16[2,256,128]{2,1,0:T(8,128)(2,1)S(1)} %copy.135), channel_id=1, source_target_pairs={{0,1},{1,2},{2,3},{3,4},{4,5},{5,6},{6,7},{7,8},{8,9},{9,10},{10,1... | collective-permute-start | bytes 393224 | tf_op jit(solution)/shard_map/while/body/eval_jaxpr/ppermute | solution.py:15
  392.4 19.9 %collective-permute-start.1 = (f32[2,256,128]{2,1,0:T(8,128)S(1)}, f32[2,256,128]{2,1,0:T(8,128)S(1)}, u32[]{:S(2)}, u32[]{:S(2)}) collective-permute-start(f32[2,256,128]{2,1,0:T(8,128)S(1)} %maximum_add_fusion.3), channel_id=1, source_target_pairs={{0,1},{1,2},{2,3},{3,4},{4,5},{5,6},{6,7},{7,8},{8,9},{9,10},{10,1... | collective-permute-start | bytes 786440 | tf_op jit(solution)/shard_map/while/body/eval_jaxpr/ppermute | solution.py:20
  417.0 15.5 %collective-permute-start.1 = (f32[2,256,128]{2,1,0:T(8,128)S(1)}, f32[2,256,128]{2,1,0:T(8,128)S(1)}, u32[]{:S(2)}, u32[]{:S(2)}) collective-permute-start(f32[2,256,128]{2,1,0:T(8,128)S(1)} %maximum_add_fusion.3), channel_id=1, source_target_pairs={{0,1},{1,2},{2,3},{3,4},{4,5},{5,6},{6,7},{7,8},{8,9},{9,10},{10,1... | collective-permute-start | bytes 786440 | tf_op jit(solution)/shard_map/while/body/eval_jaxpr/ppermute | solution.py:20
  432.5 26.2 %collective-permute-start = (bf16[2,256,128]{2,1,0:T(8,128)(2,1)S(1)}, bf16[2,256,128]{2,1,0:T(8,128)(2,1)S(1)}, u32[]{:S(2)}, u32[]{:S(2)}) collective-permute-start(bf16[2,256,128]{2,1,0:T(8,128)(2,1)S(1)} %copy.135), channel_id=1, source_target_pairs={{0,1},{1,2},{2,3},{3,4},{4,5},{5,6},{6,7},{7,8},{8,9},{9,10},{10,1... | collective-permute-start | bytes 393224 | tf_op jit(solution)/shard_map/while/body/eval_jaxpr/ppermute | solution.py:15
  451.0 17.8 %collective-permute-start.1 = (f32[2,256,128]{2,1,0:T(8,128)S(1)}, f32[2,256,128]{2,1,0:T(8,128)S(1)}, u32[]{:S(2)}, u32[]{:S(2)}) collective-permute-start(f32[2,256,128]{2,1,0:T(8,128)S(1)} %maximum_add_fusion.3), channel_id=1, source_target_pairs={{0,1},{1,2},{2,3},{3,4},{4,5},{5,6},{6,7},{7,8},{8,9},{9,10},{10,1... | collective-permute-start | bytes 786440 | tf_op jit(solution)/shard_map/while/body/eval_jaxpr/ppermute | solution.py:20
  489.7 15.8 %collective-permute-start.1 = (f32[2,256,128]{2,1,0:T(8,128)S(1)}, f32[2,256,128]{2,1,0:T(8,128)S(1)}, u32[]{:S(2)}, u32[]{:S(2)}) collective-permute-start(f32[2,256,128]{2,1,0:T(8,128)S(1)} %maximum_add_fusion.3), channel_id=1, source_target_pairs={{0,1},{1,2},{2,3},{3,4},{4,5},{5,6},{6,7},{7,8},{8,9},{9,10},{10,1... | collective-permute-start | bytes 786440 | tf_op jit(solution)/shard_map/while/body/eval_jaxpr/ppermute | solution.py:20
  523.8 21.0 %collective-permute-start = (bf16[2,256,128]{2,1,0:T(8,128)(2,1)S(1)}, bf16[2,256,128]{2,1,0:T(8,128)(2,1)S(1)}, u32[]{:S(2)}, u32[]{:S(2)}) collective-permute-start(bf16[2,256,128]{2,1,0:T(8,128)(2,1)S(1)} %copy.135), channel_id=1, source_target_pairs={{0,1},{1,2},{2,3},{3,4},{4,5},{5,6},{6,7},{7,8},{8,9},{9,10},{10,1... | collective-permute-start | bytes 393224 | tf_op jit(solution)/shard_map/while/body/eval_jaxpr/ppermute | solution.py:15
  530.7 17.4 %collective-permute-start.1 = (f32[2,256,128]{2,1,0:T(8,128)S(1)}, f32[2,256,128]{2,1,0:T(8,128)S(1)}, u32[]{:S(2)}, u32[]{:S(2)}) collective-permute-start(f32[2,256,128]{2,1,0:T(8,128)S(1)} %maximum_add_fusion.3), channel_id=1, source_target_pairs={{0,1},{1,2},{2,3},{3,4},{4,5},{5,6},{6,7},{7,8},{8,9},{9,10},{10,1... | collective-permute-start | bytes 786440 | tf_op jit(solution)/shard_map/while/body/eval_jaxpr/ppermute | solution.py:20
  548.1 19.4 %collective-permute-start = (bf16[2,256,128]{2,1,0:T(8,128)(2,1)S(1)}, bf16[2,256,128]{2,1,0:T(8,128)(2,1)S(1)}, u32[]{:S(2)}, u32[]{:S(2)}) collective-permute-start(bf16[2,256,128]{2,1,0:T(8,128)(2,1)S(1)} %copy.135), channel_id=1, source_target_pairs={{0,1},{1,2},{2,3},{3,4},{4,5},{5,6},{6,7},{7,8},{8,9},{9,10},{10,1... | collective-permute-start | bytes 393224 | tf_op jit(solution)/shard_map/while/body/eval_jaxpr/ppermute | solution.py:15
  560.2 16.3 %collective-permute-start.1 = (f32[2,256,128]{2,1,0:T(8,128)S(1)}, f32[2,256,128]{2,1,0:T(8,128)S(1)}, u32[]{:S(2)}, u32[]{:S(2)}) collective-permute-start(f32[2,256,128]{2,1,0:T(8,128)S(1)} %maximum_add_fusion.3), channel_id=1, source_target_pairs={{0,1},{1,2},{2,3},{3,4},{4,5},{5,6},{6,7},{7,8},{8,9},{9,10},{10,1... | collective-permute-start | bytes 786440 | tf_op jit(solution)/shard_map/while/body/eval_jaxpr/ppermute | solution.py:20
  576.5 15.3 %collective-permute-start = (bf16[2,256,128]{2,1,0:T(8,128)(2,1)S(1)}, bf16[2,256,128]{2,1,0:T(8,128)(2,1)S(1)}, u32[]{:S(2)}, u32[]{:S(2)}) collective-permute-start(bf16[2,256,128]{2,1,0:T(8,128)(2,1)S(1)} %copy.135), channel_id=1, source_target_pairs={{0,1},{1,2},{2,3},{3,4},{4,5},{5,6},{6,7},{7,8},{8,9},{9,10},{10,1... | collective-permute-start | bytes 393224 | tf_op jit(solution)/shard_map/while/body/eval_jaxpr/ppermute | solution.py:15
  581.3 16.5 %collective-permute-start.1 = (f32[2,256,128]{2,1,0:T(8,128)S(1)}, f32[2,256,128]{2,1,0:T(8,128)S(1)}, u32[]{:S(2)}, u32[]{:S(2)}) collective-permute-start(f32[2,256,128]{2,1,0:T(8,128)S(1)} %maximum_add_fusion.3), channel_id=1, source_target_pairs={{0,1},{1,2},{2,3},{3,4},{4,5},{5,6},{6,7},{7,8},{8,9},{9,10},{10,1... | collective-permute-start | bytes 786440 | tf_op jit(solution)/shard_map/while/body/eval_jaxpr/ppermute | solution.py:20
  597.8 17.1 %collective-permute-start = (bf16[2,256,128]{2,1,0:T(8,128)(2,1)S(1)}, bf16[2,256,128]{2,1,0:T(8,128)(2,1)S(1)}, u32[]{:S(2)}, u32[]{:S(2)}) collective-permute-start(bf16[2,256,128]{2,1,0:T(8,128)(2,1)S(1)} %copy.135), channel_id=1, source_target_pairs={{0,1},{1,2},{2,3},{3,4},{4,5},{5,6},{6,7},{7,8},{8,9},{9,10},{10,1... | collective-permute-start | bytes 393224 | tf_op jit(solution)/shard_map/while/body/eval_jaxpr/ppermute | solution.py:15
  607.6 15.5 %collective-permute-start.1 = (f32[2,256,128]{2,1,0:T(8,128)S(1)}, f32[2,256,128]{2,1,0:T(8,128)S(1)}, u32[]{:S(2)}, u32[]{:S(2)}) collective-permute-start(f32[2,256,128]{2,1,0:T(8,128)S(1)} %maximum_add_fusion.3), channel_id=1, source_target_pairs={{0,1},{1,2},{2,3},{3,4},{4,5},{5,6},{6,7},{7,8},{8,9},{9,10},{10,1... | collective-permute-start | bytes 786440 | tf_op jit(solution)/shard_map/while/body/eval_jaxpr/ppermute | solution.py:20
  623.1 17.0 %collective-permute-start = (bf16[2,256,128]{2,1,0:T(8,128)(2,1)S(1)}, bf16[2,256,128]{2,1,0:T(8,128)(2,1)S(1)}, u32[]{:S(2)}, u32[]{:S(2)}) collective-permute-start(bf16[2,256,128]{2,1,0:T(8,128)(2,1)S(1)} %copy.135), channel_id=1, source_target_pairs={{0,1},{1,2},{2,3},{3,4},{4,5},{5,6},{6,7},{7,8},{8,9},{9,10},{10,1... | collective-permute-start | bytes 393224 | tf_op jit(solution)/shard_map/while/body/eval_jaxpr/ppermute | solution.py:15
  645.1 17.3 %collective-permute-start = (bf16[2,256,128]{2,1,0:T(8,128)(2,1)S(1)}, bf16[2,256,128]{2,1,0:T(8,128)(2,1)S(1)}, u32[]{:S(2)}, u32[]{:S(2)}) collective-permute-start(bf16[2,256,128]{2,1,0:T(8,128)(2,1)S(1)} %copy.135), channel_id=1, source_target_pairs={{0,1},{1,2},{2,3},{3,4},{4,5},{5,6},{6,7},{7,8},{8,9},{9,10},{10,1... | collective-permute-start | bytes 393224 | tf_op jit(solution)/shard_map/while/body/eval_jaxpr/ppermute | solution.py:15
  654.6 15.3 %collective-permute-start.1 = (f32[2,256,128]{2,1,0:T(8,128)S(1)}, f32[2,256,128]{2,1,0:T(8,128)S(1)}, u32[]{:S(2)}, u32[]{:S(2)}) collective-permute-start(f32[2,256,128]{2,1,0:T(8,128)S(1)} %maximum_add_fusion.3), channel_id=1, source_target_pairs={{0,1},{1,2},{2,3},{3,4},{4,5},{5,6},{6,7},{7,8},{8,9},{9,10},{10,1... | collective-permute-start | bytes 786440 | tf_op jit(solution)/shard_map/while/body/eval_jaxpr/ppermute | solution.py:20
  677.7 15.6 %collective-permute-start.1 = (f32[2,256,128]{2,1,0:T(8,128)S(1)}, f32[2,256,128]{2,1,0:T(8,128)S(1)}, u32[]{:S(2)}, u32[]{:S(2)}) collective-permute-start(f32[2,256,128]{2,1,0:T(8,128)S(1)} %maximum_add_fusion.3), channel_id=1, source_target_pairs={{0,1},{1,2},{2,3},{3,4},{4,5},{5,6},{6,7},{7,8},{8,9},{9,10},{10,1... | collective-permute-start | bytes 786440 | tf_op jit(solution)/shard_map/while/body/eval_jaxpr/ppermute | solution.py:20
  697.5 17.5 %collective-permute-start.1 = (f32[2,256,128]{2,1,0:T(8,128)S(1)}, f32[2,256,128]{2,1,0:T(8,128)S(1)}, u32[]{:S(2)}, u32[]{:S(2)}) collective-permute-start(f32[2,256,128]{2,1,0:T(8,128)S(1)} %maximum_add_fusion.3), channel_id=1, source_target_pairs={{0,1},{1,2},{2,3},{3,4},{4,5},{5,6},{6,7},{7,8},{8,9},{9,10},{10,1... | collective-permute-start | bytes 786440 | tf_op jit(solution)/shard_map/while/body/eval_jaxpr/ppermute | solution.py:20
  724.5 19.5 %collective-permute-start.1 = (f32[2,256,128]{2,1,0:T(8,128)S(1)}, f32[2,256,128]{2,1,0:T(8,128)S(1)}, u32[]{:S(2)}, u32[]{:S(2)}) collective-permute-start(f32[2,256,128]{2,1,0:T(8,128)S(1)} %maximum_add_fusion.3), channel_id=1, source_target_pairs={{0,1},{1,2},{2,3},{3,4},{4,5},{5,6},{6,7},{7,8},{8,9},{9,10},{10,1... | collective-permute-start | bytes 786440 | tf_op jit(solution)/shard_map/while/body/eval_jaxpr/ppermute | solution.py:20
  747.4 15.6 %collective-permute-start.1 = (f32[2,256,128]{2,1,0:T(8,128)S(1)}, f32[2,256,128]{2,1,0:T(8,128)S(1)}, u32[]{:S(2)}, u32[]{:S(2)}) collective-permute-start(f32[2,256,128]{2,1,0:T(8,128)S(1)} %maximum_add_fusion.3), channel_id=1, source_target_pairs={{0,1},{1,2},{2,3},{3,4},{4,5},{5,6},{6,7},{7,8},{8,9},{9,10},{10,1... | collective-permute-start | bytes 786440 | tf_op jit(solution)/shard_map/while/body/eval_jaxpr/ppermute | solution.py:20
  773.1 20.8 %collective-permute-start.1 = (f32[2,256,128]{2,1,0:T(8,128)S(1)}, f32[2,256,128]{2,1,0:T(8,128)S(1)}, u32[]{:S(2)}, u32[]{:S(2)}) collective-permute-start(f32[2,256,128]{2,1,0:T(8,128)S(1)} %maximum_add_fusion.3), channel_id=1, source_target_pairs={{0,1},{1,2},{2,3},{3,4},{4,5},{5,6},{6,7},{7,8},{8,9},{9,10},{10,1... | collective-permute-start | bytes 786440 | tf_op jit(solution)/shard_map/while/body/eval_jaxpr/ppermute | solution.py:20
  811.4 49.8 %all-to-all-start.7 = ((bf16[8,32,128]{2,1,0:T(8,128)(2,1)}), bf16[8,32,128]{2,1,0:T(8,128)(2,1)S(1)}, u32[]{:S(2)}, u32[]{:S(2)}) async-start(bf16[8,32,128]{2,1,0:T(8,128)(2,1)} %bitcast.41), calls=%async_computation.7 | async-start | bytes 131072 | tf_op jit(solution)/shard_map/all_to_all | solution.py:138
  (45 other events, 528.7 us)
where the time goes:
time: 887 us; the launch traced here: 885 us
  waiting for transfers between devices  413 us (47%)
  starting transfers between devices  370 us (42%)
  matrix products  62.8 us (7%)
  local copies, waits for them, and re-layouts  23 us (3%)
  other arithmetic  11.9 us (1%)
    ppermute x32, waiting for transfers between devices, shifted(): lax.ppermute(array, axis, [(i, (i + by) % size) for i in range(size)])  351 us
    ppermute x32, starting transfers between devices, shifted(): lax.ppermute(array, axis, [(i, (i + by) % size) for i in range(size)])  146 us
    ppermute x31, starting transfers between devices, passed_along(): return lax.ppermute(array, axis, pairs)  142 us
    all_to_all x1, starting transfers between devices, local(): lax.all_to_all(key_low, 'head', split_axis=0, concat_axis=1, tiled=True)  44.8 us
  transfers between devices with their start and end apart: 72, of which 46 were waited for; matrix products, arithmetic and copies ran while one was open for 10% of the time, Pallas kernels for 0%

commit v1 on v0

--- a/solution.py
+++ b/solution.py
@@ -7,6 +7,12 @@
 KVH = 8
 HD = 128
 BLOCK = 128
+
+
+def stacked_exchange(x, axis, split, join):
+    cells = jnp.split(x, lax.axis_size(axis), axis=split)
+    got = lax.all_to_all(jnp.stack(cells), axis, 0, 0)
+    return jnp.concatenate(got, axis=join)
 
 
 def passed_along(array, axis, by):
@@ -135,7 +141,7 @@
     value_low = key_sums[1].astype(jnp.bfloat16)
     grad_query, grad_key, grad_value = (
         lax.all_to_all(query_low, "head", split_axis=0, concat_axis=1, tiled=True),
-        lax.all_to_all(key_low, "head", split_axis=0, concat_axis=1, tiled=True),
+        stacked_exchange(key_low, "head", 0, 1),
         lax.all_to_all(value_low, "head", split_axis=0, concat_axis=1, tiled=True),
     )
     return (grad_query, grad_key, grad_value)

time: 887 us -> 893 us (level)
  the two profiles are of different devices: /device:TPU:1 before, /device:TPU:16 now
where the time goes in v1:
time: 893 us; the launch traced here: 891 us
  waiting for transfers between devices  491 us (55%)
  starting transfers between devices  292 us (33%)
  matrix products  62.8 us (7%)
  local copies, waits for them, and re-layouts  27.9 us (3%)
  other arithmetic  12 us (1%)
    ppermute x32, waiting for transfers between devices, shifted(): lax.ppermute(array, axis, [(i, (i + by) % size) for i in range(size)])  244 us
    ppermute x31, waiting for transfers between devices, passed_along(): return lax.ppermute(array, axis, pairs)  187 us
    ppermute x31, starting transfers between devices, passed_along(): return lax.ppermute(array, axis, pairs)  134 us
    ppermute x32, starting transfers between devices, shifted(): lax.ppermute(array, axis, [(i, (i + by) % size) for i in range(size)])  120 us
  transfers between devices with their start and end apart: 72, of which 64 were waited for; matrix products, arithmetic and copies ran while one was open for 10% of the time, Pallas kernels for 0%

profile of v1, /device:TPU:16, one launch (start us, length us, event | category | flops | bytes accessed | tf_op | source)
XLA Modules:
  0.0 891.0 jit_solution(14437104499211950324)
XLA Ops:
  36.5 10.3 %all-to-all-done.2 = bf16[32,8,640]{2,0,1:T(8,128)(2,1)S(1)} async-done(((bf16[32,8,640]{2,0,1:T(8,128)(2,1)}), bf16[32,8,640]{2,0,1:T(8,128)(2,1)S(1)}, u32[]{:S(2)}, u32[]{:S(2)}) %all-to-all-start.2) | async-done | bytes 327712 | tf_op jit(solution)/shard_map/all_to_all | solution.py:43
  51.3 9.9 %all-to-all-done.4 = bf16[32,8,640]{2,0,1:T(8,128)(2,1)S(1)} async-done(((bf16[32,8,640]{2,0,1:T(8,128)(2,1)}), bf16[32,8,640]{2,0,1:T(8,128)(2,1)S(1)}, u32[]{:S(2)}, u32[]{:S(2)}) %all-to-all-start.4) | async-done | bytes 327712 | tf_op jit(solution)/shard_map/all_to_all | solution.py:52
  78.2 755.3 %while.20 = (s32[]{:T(128)}, bf16[2,256,128]{2,1,0:T(8,128)(2,1)S(1)}, f32[2,256,128]{2,1,0:T(8,128)S(1)}, f32[256,1,5,128]{3,0,2,1:T(8,128)S(1)}, s32[2,32]{1,0...) while((s32[]{:T(128)}, ...), condition=%wide.region_2.3_spmd.clone, body=%wide.region_0.2_spmd.clone.sunk | while | flops 422511360 | bytes 11754164 | solution.py:134
  176.0 8.6 collective-permute-start.1
  185.1 11.2 %collective-permute-done.1 = f32[2,256,128]{2,1,0:T(8,128)S(1)} collective-permute-done((f32[2,256,128]{2,1,0:T(8,128)S(1)}, f32[2,256,128]{2,1,0:T(8,128)S(1)}, u32[]{:S(2)}, u32[]{:S(2)}) %collective-permute-start.1) | collective-permute-done | bytes 262176 | tf_op jit(solution)/shard_map/while/body/eval_jaxpr/ppermute | solution.py:26
  196.3 8.4 collective-permute-start
  213.1 13.4 %collective-permute-done.1 = f32[2,256,128]{2,1,0:T(8,128)S(1)} collective-permute-done((f32[2,256,128]{2,1,0:T(8,128)S(1)}, f32[2,256,128]{2,1,0:T(8,128)S(1)}, u32[]{:S(2)}, u32[]{:S(2)}) %collective-permute-start.1) | collective-permute-done | bytes 262176 | tf_op jit(solution)/shard_map/while/body/eval_jaxpr/ppermute | solution.py:26
  235.3 11.9 %collective-permute-done = bf16[2,256,128]{2,1,0:T(8,128)(2,1)S(1)} collective-permute-done((bf16[2,256,128]{2,1,0:T(8,128)(2,1)S(1)}, bf16[2,256,128]{2,1,0:T(8,128)(2,1)S(1)}, u32[]{:S(2)}, u32[]{:S(2)}) %collective-permute-start) | collective-permute-done | bytes 131104 | tf_op jit(solution)/shard_map/while/body/eval_jaxpr/ppermute | solution.py:21
  256.0 14.4 %collective-permute-done = bf16[2,256,128]{2,1,0:T(8,128)(2,1)S(1)} collective-permute-done((bf16[2,256,128]{2,1,0:T(8,128)(2,1)S(1)}, bf16[2,256,128]{2,1,0:T(8,128)(2,1)S(1)}, u32[]{:S(2)}, u32[]{:S(2)}) %collective-permute-start) | collective-permute-done | bytes 131104 | tf_op jit(solution)/shard_map/while/body/eval_jaxpr/ppermute | solution.py:21
  280.9 13.5 %collective-permute-done = bf16[2,256,128]{2,1,0:T(8,128)(2,1)S(1)} collective-permute-done((bf16[2,256,128]{2,1,0:T(8,128)(2,1)S(1)}, bf16[2,256,128]{2,1,0:T(8,128)(2,1)S(1)}, u32[]{:S(2)}, u32[]{:S(2)}) %collective-permute-start) | collective-permute-done | bytes 131104 | tf_op jit(solution)/shard_map/while/body/eval_jaxpr/ppermute | solution.py:21
  305.4 12.9 %collective-permute-done = bf16[2,256,128]{2,1,0:T(8,128)(2,1)S(1)} collective-permute-done((bf16[2,256,128]{2,1,0:T(8,128)(2,1)S(1)}, bf16[2,256,128]{2,1,0:T(8,128)(2,1)S(1)}, u32[]{:S(2)}, u32[]{:S(2)}) %collective-permute-start) | collective-permute-done | bytes 131104 | tf_op jit(solution)/shard_map/while/body/eval_jaxpr/ppermute | solution.py:21
  329.0 13.0 %collective-permute-done = bf16[2,256,128]{2,1,0:T(8,128)(2,1)S(1)} collective-permute-done((bf16[2,256,128]{2,1,0:T(8,128)(2,1)S(1)}, bf16[2,256,128]{2,1,0:T(8,128)(2,1)S(1)}, u32[]{:S(2)}, u32[]{:S(2)}) %collective-permute-start) | collective-permute-done | bytes 131104 | tf_op jit(solution)/shard_map/while/body/eval_jaxpr/ppermute | solution.py:21
  354.1 13.8 %collective-permute-done = bf16[2,256,128]{2,1,0:T(8,128)(2,1)S(1)} collective-permute-done((bf16[2,256,128]{2,1,0:T(8,128)(2,1)S(1)}, bf16[2,256,128]{2,1,0:T(8,128)(2,1)S(1)}, u32[]{:S(2)}, u32[]{:S(2)}) %collective-permute-start) | collective-permute-done | bytes 131104 | tf_op jit(solution)/shard_map/while/body/eval_jaxpr/ppermute | solution.py:21
  375.5 9.2 %collective-permute-done = bf16[2,256,128]{2,1,0:T(8,128)(2,1)S(1)} collective-permute-done((bf16[2,256,128]{2,1,0:T(8,128)(2,1)S(1)}, bf16[2,256,128]{2,1,0:T(8,128)(2,1)S(1)}, u32[]{:S(2)}, u32[]{:S(2)}) %collective-permute-start) | collective-permute-done | bytes 131104 | tf_op jit(solution)/shard_map/while/body/eval_jaxpr/ppermute | solution.py:21
  429.8 8.9 %collective-permute-done.1 = f32[2,256,128]{2,1,0:T(8,128)S(1)} collective-permute-done((f32[2,256,128]{2,1,0:T(8,128)S(1)}, f32[2,256,128]{2,1,0:T(8,128)S(1)}, u32[]{:S(2)}, u32[]{:S(2)}) %collective-permute-start.1) | collective-permute-done | bytes 262176 | tf_op jit(solution)/shard_map/while/body/eval_jaxpr/ppermute | solution.py:26
  523.2 9.6 %collective-permute-done.1 = f32[2,256,128]{2,1,0:T(8,128)S(1)} collective-permute-done((f32[2,256,128]{2,1,0:T(8,128)S(1)}, f32[2,256,128]{2,1,0:T(8,128)S(1)}, u32[]{:S(2)}, u32[]{:S(2)}) %collective-permute-start.1) | collective-permute-done | bytes 262176 | tf_op jit(solution)/shard_map/while/body/eval_jaxpr/ppermute | solution.py:26
  532.8 8.4 collective-permute-start
  543.2 11.4 %collective-permute-start.1 = (f32[2,256,128]{2,1,0:T(8,128)S(1)}, f32[2,256,128]{2,1,0:T(8,128)S(1)}, u32[]{:S(2)}, u32[]{:S(2)}) collective-permute-start(f32[2,256,128]{2,1,0:T(8,128)S(1)} %maximum_add_fusion.3), channel_id=1, source_target_pairs={{0,1},{1,2},{2,3},{3,4},{4,5},{5,6},{6,7},{7,8},{8,9},{9,10},{10,1... | collective-permute-start | bytes 786440 | tf_op jit(solution)/shard_map/while/body/eval_jaxpr/ppermute | solution.py:26
  555.1 9.7 %collective-permute-done.1 = f32[2,256,128]{2,1,0:T(8,128)S(1)} collective-permute-done((f32[2,256,128]{2,1,0:T(8,128)S(1)}, f32[2,256,128]{2,1,0:T(8,128)S(1)}, u32[]{:S(2)}, u32[]{:S(2)}) %collective-permute-start.1) | collective-permute-done | bytes 262176 | tf_op jit(solution)/shard_map/while/body/eval_jaxpr/ppermute | solution.py:26
  564.8 8.4 collective-permute-start
  579.0 12.8 %collective-permute-done.1 = f32[2,256,128]{2,1,0:T(8,128)S(1)} collective-permute-done((f32[2,256,128]{2,1,0:T(8,128)S(1)}, f32[2,256,128]{2,1,0:T(8,128)S(1)}, u32[]{:S(2)}, u32[]{:S(2)}) %collective-permute-start.1) | collective-permute-done | bytes 262176 | tf_op jit(solution)/shard_map/while/body/eval_jaxpr/ppermute | solution.py:26
  616.2 8.3 collective-permute-start
  633.8 9.3 %collective-permute-done.1 = f32[2,256,128]{2,1,0:T(8,128)S(1)} collective-permute-done((f32[2,256,128]{2,1,0:T(8,128)S(1)}, f32[2,256,128]{2,1,0:T(8,128)S(1)}, u32[]{:S(2)}, u32[]{:S(2)}) %collective-permute-start.1) | collective-permute-done | bytes 262176 | tf_op jit(solution)/shard_map/while/body/eval_jaxpr/ppermute | solution.py:26
  657.0 9.8 %collective-permute-done.1 = f32[2,256,128]{2,1,0:T(8,128)S(1)} collective-permute-done((f32[2,256,128]{2,1,0:T(8,128)S(1)}, f32[2,256,128]{2,1,0:T(8,128)S(1)}, u32[]{:S(2)}, u32[]{:S(2)}) %collective-permute-start.1) | collective-permute-done | bytes 262176 | tf_op jit(solution)/shard_map/while/body/eval_jaxpr/ppermute | solution.py:26
  704.7 16.5 %collective-permute-done.1 = f32[2,256,128]{2,1,0:T(8,128)S(1)} collective-permute-done((f32[2,256,128]{2,1,0:T(8,128)S(1)}, f32[2,256,128]{2,1,0:T(8,128)S(1)}, u32[]{:S(2)}, u32[]{:S(2)}) %collective-permute-start.1) | collective-permute-done | bytes 262176 | tf_op jit(solution)/shard_map/while/body/eval_jaxpr/ppermute | solution.py:26
  747.4 10.7 %collective-permute-done = bf16[2,256,128]{2,1,0:T(8,128)(2,1)S(1)} collective-permute-done((bf16[2,256,128]{2,1,0:T(8,128)(2,1)S(1)}, bf16[2,256,128]{2,1,0:T(8,128)(2,1)S(1)}, u32[]{:S(2)}, u32[]{:S(2)}) %collective-permute-start) | collective-permute-done | bytes 131104 | tf_op jit(solution)/shard_map/while/body/eval_jaxpr/ppermute | solution.py:21
  765.5 14.0 %collective-permute-done = bf16[2,256,128]{2,1,0:T(8,128)(2,1)S(1)} collective-permute-done((bf16[2,256,128]{2,1,0:T(8,128)(2,1)S(1)}, bf16[2,256,128]{2,1,0:T(8,128)(2,1)S(1)}, u32[]{:S(2)}, u32[]{:S(2)}) %collective-permute-start) | collective-permute-done | bytes 131104 | tf_op jit(solution)/shard_map/while/body/eval_jaxpr/ppermute | solution.py:21
  779.5 8.7 collective-permute-done.1
  792.8 11.0 %collective-permute-done = bf16[2,256,128]{2,1,0:T(8,128)(2,1)S(1)} collective-permute-done((bf16[2,256,128]{2,1,0:T(8,128)(2,1)S(1)}, bf16[2,256,128]{2,1,0:T(8,128)(2,1)S(1)}, u32[]{:S(2)}, u32[]{:S(2)}) %collective-permute-start) | collective-permute-done | bytes 131104 | tf_op jit(solution)/shard_map/while/body/eval_jaxpr/ppermute | solution.py:21
  814.8 12.5 %collective-permute-done = bf16[2,256,128]{2,1,0:T(8,128)(2,1)S(1)} collective-permute-done((bf16[2,256,128]{2,1,0:T(8,128)(2,1)S(1)}, bf16[2,256,128]{2,1,0:T(8,128)(2,1)S(1)}, u32[]{:S(2)}, u32[]{:S(2)}) %collective-permute-start) | collective-permute-done | bytes 131104 | tf_op jit(solution)/shard_map/while/body/eval_jaxpr/ppermute | solution.py:21
  836.8 11.9 %collective-permute-done.2 = bf16[2,256,128]{2,1,0:T(8,128)(2,1)S(1)} collective-permute-done((bf16[2,256,128]{2,1,0:T(8,128)(2,1)S(1)}, bf16[2,256,128]{2,1,0:T(8,128)(2,1)S(1)}, u32[]{:S(2)}, u32[]{:S(2)}) %collective-permute-start.2) | collective-permute-done | bytes 131104 | tf_op jit(solution)/shard_map/ppermute | solution.py:26
  880.5 9.8 %all-to-all-done.6 = bf16[8,32,640]{2,1,0:T(8,128)(2,1)S(1)} async-done(((bf16[8,32,640]{2,1,0:T(8,128)(2,1)}), bf16[8,32,640]{2,1,0:T(8,128)(2,1)S(1)}, u32[]{:S(2)}, u32[]{:S(2)}) %all-to-all-start.6) | async-done | bytes 327712 | tf_op jit(solution)/shard_map/all_to_all | solution.py:143
  (642 shorter events, 543.9 us)
Async XLA Ops:
  78.3 17.7 %collective-permute-start = (bf16[2,256,128]{2,1,0:T(8,128)(2,1)S(1)}, bf16[2,256,128]{2,1,0:T(8,128)(2,1)S(1)}, u32[]{:S(2)}, u32[]{:S(2)}) collective-permute-start(bf16[2,256,128]{2,1,0:T(8,128)(2,1)S(1)} %copy.134), channel_id=1, source_target_pairs={{0,1},{1,2},{2,3},{3,4},{4,5},{5,6},{6,7},{7,8},{8,9},{9,10},{10,1... | collective-permute-start | bytes 393224 | tf_op jit(solution)/shard_map/while/body/eval_jaxpr/ppermute | solution.py:21
  86.8 17.3 %collective-permute-start.1 = (f32[2,256,128]{2,1,0:T(8,128)S(1)}, f32[2,256,128]{2,1,0:T(8,128)S(1)}, u32[]{:S(2)}, u32[]{:S(2)}) collective-permute-start(f32[2,256,128]{2,1,0:T(8,128)S(1)} %maximum_add_fusion.3), channel_id=1, source_target_pairs={{0,1},{1,2},{2,3},{3,4},{4,5},{5,6},{6,7},{7,8},{8,9},{9,10},{10,1... | collective-permute-start | bytes 786440 | tf_op jit(solution)/shard_map/while/body/eval_jaxpr/ppermute | solution.py:26
  176.0 20.3 %collective-permute-start.1 = (f32[2,256,128]{2,1,0:T(8,128)S(1)}, f32[2,256,128]{2,1,0:T(8,128)S(1)}, u32[]{:S(2)}, u32[]{:S(2)}) collective-permute-start(f32[2,256,128]{2,1,0:T(8,128)S(1)} %maximum_add_fusion.3), channel_id=1, source_target_pairs={{0,1},{1,2},{2,3},{3,4},{4,5},{5,6},{6,7},{7,8},{8,9},{9,10},{10,1... | collective-permute-start | bytes 786440 | tf_op jit(solution)/shard_map/while/body/eval_jaxpr/ppermute | solution.py:26
  206.7 19.8 %collective-permute-start.1 = (f32[2,256,128]{2,1,0:T(8,128)S(1)}, f32[2,256,128]{2,1,0:T(8,128)S(1)}, u32[]{:S(2)}, u32[]{:S(2)}) collective-permute-start(f32[2,256,128]{2,1,0:T(8,128)S(1)} %maximum_add_fusion.3), channel_id=1, source_target_pairs={{0,1},{1,2},{2,3},{3,4},{4,5},{5,6},{6,7},{7,8},{8,9},{9,10},{10,1... | collective-permute-start | bytes 786440 | tf_op jit(solution)/shard_map/while/body/eval_jaxpr/ppermute | solution.py:26
  226.5 20.7 %collective-permute-start = (bf16[2,256,128]{2,1,0:T(8,128)(2,1)S(1)}, bf16[2,256,128]{2,1,0:T(8,128)(2,1)S(1)}, u32[]{:S(2)}, u32[]{:S(2)}) collective-permute-start(bf16[2,256,128]{2,1,0:T(8,128)(2,1)S(1)} %copy.134), channel_id=1, source_target_pairs={{0,1},{1,2},{2,3},{3,4},{4,5},{5,6},{6,7},{7,8},{8,9},{9,10},{10,1... | collective-permute-start | bytes 393224 | tf_op jit(solution)/shard_map/while/body/eval_jaxpr/ppermute | solution.py:21
  230.5 20.8 %collective-permute-start.1 = (f32[2,256,128]{2,1,0:T(8,128)S(1)}, f32[2,256,128]{2,1,0:T(8,128)S(1)}, u32[]{:S(2)}, u32[]{:S(2)}) collective-permute-start(f32[2,256,128]{2,1,0:T(8,128)S(1)} %maximum_add_fusion.3), channel_id=1, source_target_pairs={{0,1},{1,2},{2,3},{3,4},{4,5},{5,6},{6,7},{7,8},{8,9},{9,10},{10,1... | collective-permute-start | bytes 786440 | tf_op jit(solution)/shard_map/while/body/eval_jaxpr/ppermute | solution.py:26
  251.4 19.0 %collective-permute-start = (bf16[2,256,128]{2,1,0:T(8,128)(2,1)S(1)}, bf16[2,256,128]{2,1,0:T(8,128)(2,1)S(1)}, u32[]{:S(2)}, u32[]{:S(2)}) collective-permute-start(bf16[2,256,128]{2,1,0:T(8,128)(2,1)S(1)} %copy.134), channel_id=1, source_target_pairs={{0,1},{1,2},{2,3},{3,4},{4,5},{5,6},{6,7},{7,8},{8,9},{9,10},{10,1... | collective-permute-start | bytes 393224 | tf_op jit(solution)/shard_map/while/body/eval_jaxpr/ppermute | solution.py:21
  255.3 20.5 %collective-permute-start.1 = (f32[2,256,128]{2,1,0:T(8,128)S(1)}, f32[2,256,128]{2,1,0:T(8,128)S(1)}, u32[]{:S(2)}, u32[]{:S(2)}) collective-permute-start(f32[2,256,128]{2,1,0:T(8,128)S(1)} %maximum_add_fusion.3), channel_id=1, source_target_pairs={{0,1},{1,2},{2,3},{3,4},{4,5},{5,6},{6,7},{7,8},{8,9},{9,10},{10,1... | collective-permute-start | bytes 786440 | tf_op jit(solution)/shard_map/while/body/eval_jaxpr/ppermute | solution.py:26
  275.8 18.6 %collective-permute-start = (bf16[2,256,128]{2,1,0:T(8,128)(2,1)S(1)}, bf16[2,256,128]{2,1,0:T(8,128)(2,1)S(1)}, u32[]{:S(2)}, u32[]{:S(2)}) collective-permute-start(bf16[2,256,128]{2,1,0:T(8,128)(2,1)S(1)} %copy.134), channel_id=1, source_target_pairs={{0,1},{1,2},{2,3},{3,4},{4,5},{5,6},{6,7},{7,8},{8,9},{9,10},{10,1... | collective-permute-start | bytes 393224 | tf_op jit(solution)/shard_map/while/body/eval_jaxpr/ppermute | solution.py:21
  280.2 20.6 %collective-permute-start.1 = (f32[2,256,128]{2,1,0:T(8,128)S(1)}, f32[2,256,128]{2,1,0:T(8,128)S(1)}, u32[]{:S(2)}, u32[]{:S(2)}) collective-permute-start(f32[2,256,128]{2,1,0:T(8,128)S(1)} %maximum_add_fusion.3), channel_id=1, source_target_pairs={{0,1},{1,2},{2,3},{3,4},{4,5},{5,6},{6,7},{7,8},{8,9},{9,10},{10,1... | collective-permute-start | bytes 786440 | tf_op jit(solution)/shard_map/while/body/eval_jaxpr/ppermute | solution.py:26
  300.8 17.5 %collective-permute-start = (bf16[2,256,128]{2,1,0:T(8,128)(2,1)S(1)}, bf16[2,256,128]{2,1,0:T(8,128)(2,1)S(1)}, u32[]{:S(2)}, u32[]{:S(2)}) collective-permute-start(bf16[2,256,128]{2,1,0:T(8,128)(2,1)S(1)} %copy.134), channel_id=1, source_target_pairs={{0,1},{1,2},{2,3},{3,4},{4,5},{5,6},{6,7},{7,8},{8,9},{9,10},{10,1... | collective-permute-start | bytes 393224 | tf_op jit(solution)/shard_map/while/body/eval_jaxpr/ppermute | solution.py:21
  304.8 19.5 %collective-permute-start.1 = (f32[2,256,128]{2,1,0:T(8,128)S(1)}, f32[2,256,128]{2,1,0:T(8,128)S(1)}, u32[]{:S(2)}, u32[]{:S(2)}) collective-permute-start(f32[2,256,128]{2,1,0:T(8,128)S(1)} %maximum_add_fusion.3), channel_id=1, source_target_pairs={{0,1},{1,2},{2,3},{3,4},{4,5},{5,6},{6,7},{7,8},{8,9},{9,10},{10,1... | collective-permute-start | bytes 786440 | tf_op jit(solution)/shard_map/while/body/eval_jaxpr/ppermute | solution.py:26
  324.2 17.7 %collective-permute-start = (bf16[2,256,128]{2,1,0:T(8,128)(2,1)S(1)}, bf16[2,256,128]{2,1,0:T(8,128)(2,1)S(1)}, u32[]{:S(2)}, u32[]{:S(2)}) collective-permute-start(bf16[2,256,128]{2,1,0:T(8,128)(2,1)S(1)} %copy.134), channel_id=1, source_target_pairs={{0,1},{1,2},{2,3},{3,4},{4,5},{5,6},{6,7},{7,8},{8,9},{9,10},{10,1... | collective-permute-start | bytes 393224 | tf_op jit(solution)/shard_map/while/body/eval_jaxpr/ppermute | solution.py:21
  328.3 21.2 %collective-permute-start.1 = (f32[2,256,128]{2,1,0:T(8,128)S(1)}, f32[2,256,128]{2,1,0:T(8,128)S(1)}, u32[]{:S(2)}, u32[]{:S(2)}) collective-permute-start(f32[2,256,128]{2,1,0:T(8,128)S(1)} %maximum_add_fusion.3), channel_id=1, source_target_pairs={{0,1},{1,2},{2,3},{3,4},{4,5},{5,6},{6,7},{7,8},{8,9},{9,10},{10,1... | collective-permute-start | bytes 786440 | tf_op jit(solution)/shard_map/while/body/eval_jaxpr/ppermute | solution.py:26
  349.5 18.5 %collective-permute-start = (bf16[2,256,128]{2,1,0:T(8,128)(2,1)S(1)}, bf16[2,256,128]{2,1,0:T(8,128)(2,1)S(1)}, u32[]{:S(2)}, u32[]{:S(2)}) collective-permute-start(bf16[2,256,128]{2,1,0:T(8,128)(2,1)S(1)} %copy.134), channel_id=1, source_target_pairs={{0,1},{1,2},{2,3},{3,4},{4,5},{5,6},{6,7},{7,8},{8,9},{9,10},{10,1... | collective-permute-start | bytes 393224 | tf_op jit(solution)/shard_map/while/body/eval_jaxpr/ppermute | solution.py:21
  353.5 17.4 %collective-permute-start.1 = (f32[2,256,128]{2,1,0:T(8,128)S(1)}, f32[2,256,128]{2,1,0:T(8,128)S(1)}, u32[]{:S(2)}, u32[]{:S(2)}) collective-permute-start(f32[2,256,128]{2,1,0:T(8,128)S(1)} %maximum_add_fusion.3), channel_id=1, source_target_pairs={{0,1},{1,2},{2,3},{3,4},{4,5},{5,6},{6,7},{7,8},{8,9},{9,10},{10,1... | collective-permute-start | bytes 786440 | tf_op jit(solution)/shard_map/while/body/eval_jaxpr/ppermute | solution.py:26
  389.1 18.0 %collective-permute-start = (bf16[2,256,128]{2,1,0:T(8,128)(2,1)S(1)}, bf16[2,256,128]{2,1,0:T(8,128)(2,1)S(1)}, u32[]{:S(2)}, u32[]{:S(2)}) collective-permute-start(bf16[2,256,128]{2,1,0:T(8,128)(2,1)S(1)} %copy.134), channel_id=1, source_target_pairs={{0,1},{1,2},{2,3},{3,4},{4,5},{5,6},{6,7},{7,8},{8,9},{9,10},{10,1... | collective-permute-start | bytes 393224 | tf_op jit(solution)/shard_map/while/body/eval_jaxpr/ppermute | solution.py:21
  411.3 18.5 %collective-permute-start = (bf16[2,256,128]{2,1,0:T(8,128)(2,1)S(1)}, bf16[2,256,128]{2,1,0:T(8,128)(2,1)S(1)}, u32[]{:S(2)}, u32[]{:S(2)}) collective-permute-start(bf16[2,256,128]{2,1,0:T(8,128)(2,1)S(1)} %copy.134), channel_id=1, source_target_pairs={{0,1},{1,2},{2,3},{3,4},{4,5},{5,6},{6,7},{7,8},{8,9},{9,10},{10,1... | collective-permute-start | bytes 393224 | tf_op jit(solution)/shard_map/while/body/eval_jaxpr/ppermute | solution.py:21
  421.1 17.7 %collective-permute-start.1 = (f32[2,256,128]{2,1,0:T(8,128)S(1)}, f32[2,256,128]{2,1,0:T(8,128)S(1)}, u32[]{:S(2)}, u32[]{:S(2)}) collective-permute-start(f32[2,256,128]{2,1,0:T(8,128)S(1)} %maximum_add_fusion.3), channel_id=1, source_target_pairs={{0,1},{1,2},{2,3},{3,4},{4,5},{5,6},{6,7},{7,8},{8,9},{9,10},{10,1... | collective-permute-start | bytes 786440 | tf_op jit(solution)/shard_map/while/body/eval_jaxpr/ppermute | solution.py:26
  532.8 22.3 %collective-permute-start = (bf16[2,256,128]{2,1,0:T(8,128)(2,1)S(1)}, bf16[2,256,128]{2,1,0:T(8,128)(2,1)S(1)}, u32[]{:S(2)}, u32[]{:S(2)}) collective-permute-start(bf16[2,256,128]{2,1,0:T(8,128)(2,1)S(1)} %copy.134), channel_id=1, source_target_pairs={{0,1},{1,2},{2,3},{3,4},{4,5},{5,6},{6,7},{7,8},{8,9},{9,10},{10,1... | collective-permute-start | bytes 393224 | tf_op jit(solution)/shard_map/while/body/eval_jaxpr/ppermute | solution.py:21
  543.2 21.6 %collective-permute-start.1 = (f32[2,256,128]{2,1,0:T(8,128)S(1)}, f32[2,256,128]{2,1,0:T(8,128)S(1)}, u32[]{:S(2)}, u32[]{:S(2)}) collective-permute-start(f32[2,256,128]{2,1,0:T(8,128)S(1)} %maximum_add_fusion.3), channel_id=1, source_target_pairs={{0,1},{1,2},{2,3},{3,4},{4,5},{5,6},{6,7},{7,8},{8,9},{9,10},{10,1... | collective-permute-start | bytes 786440 | tf_op jit(solution)/shard_map/while/body/eval_jaxpr/ppermute | solution.py:26
  595.8 20.4 %collective-permute-start.1 = (f32[2,256,128]{2,1,0:T(8,128)S(1)}, f32[2,256,128]{2,1,0:T(8,128)S(1)}, u32[]{:S(2)}, u32[]{:S(2)}) collective-permute-start(f32[2,256,128]{2,1,0:T(8,128)S(1)} %maximum_add_fusion.3), channel_id=1, source_target_pairs={{0,1},{1,2},{2,3},{3,4},{4,5},{5,6},{6,7},{7,8},{8,9},{9,10},{10,1... | collective-permute-start | bytes 786440 | tf_op jit(solution)/shard_map/while/body/eval_jaxpr/ppermute | solution.py:26
  616.2 17.5 %collective-permute-start = (bf16[2,256,128]{2,1,0:T(8,128)(2,1)S(1)}, bf16[2,256,128]{2,1,0:T(8,128)(2,1)S(1)}, u32[]{:S(2)}, u32[]{:S(2)}) collective-permute-start(bf16[2,256,128]{2,1,0:T(8,128)(2,1)S(1)} %copy.134), channel_id=1, source_target_pairs={{0,1},{1,2},{2,3},{3,4},{4,5},{5,6},{6,7},{7,8},{8,9},{9,10},{10,1... | collective-permute-start | bytes 393224 | tf_op jit(solution)/shard_map/while/body/eval_jaxpr/ppermute | solution.py:21
  649.6 17.2 %collective-permute-start.1 = (f32[2,256,128]{2,1,0:T(8,128)S(1)}, f32[2,256,128]{2,1,0:T(8,128)S(1)}, u32[]{:S(2)}, u32[]{:S(2)}) collective-permute-start(f32[2,256,128]{2,1,0:T(8,128)S(1)} %maximum_add_fusion.3), channel_id=1, source_target_pairs={{0,1},{1,2},{2,3},{3,4},{4,5},{5,6},{6,7},{7,8},{8,9},{9,10},{10,1... | collective-permute-start | bytes 786440 | tf_op jit(solution)/shard_map/while/body/eval_jaxpr/ppermute | solution.py:26
  666.8 17.4 %collective-permute-start = (bf16[2,256,128]{2,1,0:T(8,128)(2,1)S(1)}, bf16[2,256,128]{2,1,0:T(8,128)(2,1)S(1)}, u32[]{:S(2)}, u32[]{:S(2)}) collective-permute-start(bf16[2,256,128]{2,1,0:T(8,128)(2,1)S(1)} %copy.134), channel_id=1, source_target_pairs={{0,1},{1,2},{2,3},{3,4},{4,5},{5,6},{6,7},{7,8},{8,9},{9,10},{10,1... | collective-permute-start | bytes 393224 | tf_op jit(solution)/shard_map/while/body/eval_jaxpr/ppermute | solution.py:21
  671.6 17.5 %collective-permute-start.1 = (f32[2,256,128]{2,1,0:T(8,128)S(1)}, f32[2,256,128]{2,1,0:T(8,128)S(1)}, u32[]{:S(2)}, u32[]{:S(2)}) collective-permute-start(f32[2,256,128]{2,1,0:T(8,128)S(1)} %maximum_add_fusion.3), channel_id=1, source_target_pairs={{0,1},{1,2},{2,3},{3,4},{4,5},{5,6},{6,7},{7,8},{8,9},{9,10},{10,1... | collective-permute-start | bytes 786440 | tf_op jit(solution)/shard_map/while/body/eval_jaxpr/ppermute | solution.py:26
  699.1 22.1 %collective-permute-start.1 = (f32[2,256,128]{2,1,0:T(8,128)S(1)}, f32[2,256,128]{2,1,0:T(8,128)S(1)}, u32[]{:S(2)}, u32[]{:S(2)}) collective-permute-start(f32[2,256,128]{2,1,0:T(8,128)S(1)} %maximum_add_fusion.3), channel_id=1, source_target_pairs={{0,1},{1,2},{2,3},{3,4},{4,5},{5,6},{6,7},{7,8},{8,9},{9,10},{10,1... | collective-permute-start | bytes 786440 | tf_op jit(solution)/shard_map/while/body/eval_jaxpr/ppermute | solution.py:26
  760.9 18.6 %collective-permute-start = (bf16[2,256,128]{2,1,0:T(8,128)(2,1)S(1)}, bf16[2,256,128]{2,1,0:T(8,128)(2,1)S(1)}, u32[]{:S(2)}, u32[]{:S(2)}) collective-permute-start(bf16[2,256,128]{2,1,0:T(8,128)(2,1)S(1)} %copy.134), channel_id=1, source_target_pairs={{0,1},{1,2},{2,3},{3,4},{4,5},{5,6},{6,7},{7,8},{8,9},{9,10},{10,1... | collective-permute-start | bytes 393224 | tf_op jit(solution)/shard_map/while/body/eval_jaxpr/ppermute | solution.py:21
  764.9 23.4 %collective-permute-start.1 = (f32[2,256,128]{2,1,0:T(8,128)S(1)}, f32[2,256,128]{2,1,0:T(8,128)S(1)}, u32[]{:S(2)}, u32[]{:S(2)}) collective-permute-start(f32[2,256,128]{2,1,0:T(8,128)S(1)} %maximum_add_fusion.3), channel_id=1, source_target_pairs={{0,1},{1,2},{2,3},{3,4},{4,5},{5,6},{6,7},{7,8},{8,9},{9,10},{10,1... | collective-permute-start | bytes 786440 | tf_op jit(solution)/shard_map/while/body/eval_jaxpr/ppermute | solution.py:26
  792.2 18.0 %collective-permute-start.1 = (f32[2,256,128]{2,1,0:T(8,128)S(1)}, f32[2,256,128]{2,1,0:T(8,128)S(1)}, u32[]{:S(2)}, u32[]{:S(2)}) collective-permute-start(f32[2,256,128]{2,1,0:T(8,128)S(1)} %maximum_add_fusion.3), channel_id=1, source_target_pairs={{0,1},{1,2},{2,3},{3,4},{4,5},{5,6},{6,7},{7,8},{8,9},{9,10},{10,1... | collective-permute-start | bytes 786440 | tf_op jit(solution)/shard_map/while/body/eval_jaxpr/ppermute | solution.py:26
  810.2 17.1 %collective-permute-start = (bf16[2,256,128]{2,1,0:T(8,128)(2,1)S(1)}, bf16[2,256,128]{2,1,0:T(8,128)(2,1)S(1)}, u32[]{:S(2)}, u32[]{:S(2)}) collective-permute-start(bf16[2,256,128]{2,1,0:T(8,128)(2,1)S(1)} %copy.134), channel_id=1, source_target_pairs={{0,1},{1,2},{2,3},{3,4},{4,5},{5,6},{6,7},{7,8},{8,9},{9,10},{10,1... | collective-permute-start | bytes 393224 | tf_op jit(solution)/shard_map/while/body/eval_jaxpr/ppermute | solution.py:21
  814.1 19.4 %collective-permute-start.1 = (f32[2,256,128]{2,1,0:T(8,128)S(1)}, f32[2,256,128]{2,1,0:T(8,128)S(1)}, u32[]{:S(2)}, u32[]{:S(2)}) collective-permute-start(f32[2,256,128]{2,1,0:T(8,128)S(1)} %maximum_add_fusion.3), channel_id=1, source_target_pairs={{0,1},{1,2},{2,3},{3,4},{4,5},{5,6},{6,7},{7,8},{8,9},{9,10},{10,1... | collective-permute-start | bytes 786440 | tf_op jit(solution)/shard_map/while/body/eval_jaxpr/ppermute | solution.py:26
  (45 other events, 675.0 us)
